TPU v7x, 512 devices: a whole 4x4x16 slice. The times are simulated.
512 devices in a mesh: grp: 16 (over z), cube: 32 (over y, x, core).
Axes of the slice: x: 4, y: 4, z: 16, core: 2. Of those that a mesh axis runs over, the one named last changes fastest.
Arguments:
- density: float32 [16, 32, 64, 512], P('grp', 'cube'), may hold values from 0.5 to 2
- momentum: float32 [16, 32, 3, 64, 512], P('grp', 'cube'), may hold values from -3 to 3
- element_size: float32 [16, 32, 3, 64], P('grp', 'cube'), may hold values from 0.5 to 2
- section_slots: int32 [16, 32, 5, 1024], P('grp', 'cube'), may hold values from 0 to 28671, as said below
- section_counts: int32 [16, 32, 5], P('grp', 'cube'), may hold values from 512 to 1024, as said below
- cross_slots: int32 [16, 32, 2, 1024], P('grp', 'cube'), may hold values from 0 to 28671, as said below
- cross_counts: int32 [16, 32, 2], P('grp', 'cube'), may hold values from 512 to 1024, as said below
Outputs:
- new_density: float32 [16, 32, 64, 512], P('grp', 'cube')
- new_momentum: float32 [16, 32, 3, 64, 512], P('grp', 'cube')
Inputs may be any that keep to these rules, and one draw needn't show every extreme that they name: All slots of a device, of section_slots and cross_slots together, name different nodes. `section_counts`: the two devices of a pair have the same count for that bit; some pair fills all 1024 slots. All slots of a device, of section_slots and cross_slots together, name different nodes. `cross_counts`: a device's count toward the upper group equals the upper device's count toward the lower group; some pair fills all 1024 slots.
All inputs are finite; a program needn't handle non-finite values.
Results may differ from a plain program's by a relative error of at most 0.0003.
Values sent between devices are 32-bit elements; how exact they have to be, the bound alone decides.
No kernel may reach another device: no remote copies, remote signals or barrier semaphores. Data moves between devices by JAX's collectives and lax.ppermute only.
A program may use at most 64 MiB of HBM per device.

v0:
```python
import jax
import jax.numpy as jnp
import numpy as np
from jax import lax
from jax.sharding import PartitionSpec as P

GAMMA = 1.4
DT = 0.01
ORDER = 7


def with_halo(cells, sides, width):
    for axis, dim in sides:
        count = lax.axis_size(axis)
        head = lax.slice_in_dim(cells, 0, width, axis=dim)
        tail = lax.slice_in_dim(cells, cells.shape[dim] - width, cells.shape[dim], axis=dim)
        cells = jnp.concatenate(
            [
                lax.ppermute(tail, axis, [(i, (i + 1) % count) for i in range(count)]),
                cells,
                lax.ppermute(head, axis, [((i + 1) % count, i) for i in range(count)]),
            ],
            axis=dim,
        )
    return cells


def gll_tables():
    points = np.array(
        [
            -1.0,
            -0.8717401485096066,
            -0.5917001814331423,
            -0.2092992179024789,
            0.2092992179024789,
            0.5917001814331423,
            0.8717401485096066,
            1.0,
        ]
    )
    weights = np.array(
        [
            1.0 / 28.0,
            0.2107042271435061,
            0.3411226924835044,
            0.4124587946587038,
            0.4124587946587038,
            0.3411226924835044,
            0.2107042271435061,
            1.0 / 28.0,
        ]
    )
    previous = np.ones(8)
    current = points.copy()
    for order_now in range(1, ORDER):
        following = ((2 * order_now + 1) * points * current - order_now * previous) / (
            order_now + 1
        )
        previous = current
        current = following
    derivative = np.zeros((8, 8))
    for i in range(8):
        for j in range(8):
            if i != j:
                derivative[i, j] = current[i] / (current[j] * (points[i] - points[j]))
    derivative[0, 0] = -ORDER * (ORDER + 1) / 4.0
    derivative[7, 7] = ORDER * (ORDER + 1) / 4.0
    return (points, weights, derivative)


def derivative_tables():
    points, weights, derivative = gll_tables()
    eye_eight = np.eye(8)
    eye_wide = np.eye(64)
    along_first = np.kron(derivative, eye_wide)
    along_second = np.kron(eye_eight, np.kron(derivative, eye_eight))
    along_third = np.kron(eye_wide, derivative)
    tables = [jnp.asarray(t.T, jnp.float32) for t in (along_first, along_second, along_third)]
    node_weight = jnp.asarray(np.kron(weights, np.kron(weights, weights)), jnp.float32)
    return (tables, node_weight)


def split_onehots(row_ids, high_count):
    high_part = (row_ids[:, None] // 128 == jnp.arange(high_count, dtype=jnp.int32)[None]).astype(
        jnp.float32
    )
    low_part = (row_ids[:, None] % 128 == jnp.arange(128, dtype=jnp.int32)[None]).astype(
        jnp.float32
    )
    return (high_part, low_part)


def pick_rows(table, slot_ids, counts):
    high_count = table.shape[0]
    flat_table = table.reshape(high_count, 640)

    def pick_one_row(pieces):
        row_ids, count = pieces
        high_part, low_part = split_onehots(row_ids, high_count)
        rows_high = jnp.dot(high_part, flat_table, precision=lax.Precision.HIGHEST).reshape(
            -1, 5, 128
        )
        picked = jnp.sum(rows_high * low_part[:, None, :], axis=2)
        live_mask = (jnp.arange(row_ids.shape[0]) < count).astype(jnp.float32)
        return (picked * live_mask[:, None]).T

    return jnp.moveaxis(lax.map(pick_one_row, (slot_ids, counts)), 0, 1)


def add_rows(table, slot_ids, incoming):
    high_count = table.shape[0]

    def add_one_row(carry, pieces):
        row_ids, values = pieces
        high_part, low_part = split_onehots(row_ids, high_count)
        spread = (values.T[:, :, None] * low_part[:, None, :]).reshape(-1, 640)
        added = lax.dot_general(
            high_part, spread, (((0,), (0,)), ((), ())), precision=lax.Precision.HIGHEST
        )
        return (carry + added, None)

    flat_table, unused = lax.scan(
        add_one_row, table.reshape(high_count, 640), (slot_ids, jnp.moveaxis(incoming, 1, 0))
    )
    return flat_table.reshape(high_count, 5, 128)


def local(
    density, momentum, element_size, section_slots, section_counts, cross_slots, cross_counts
):
    mass_density = density[0, 0]
    moment = momentum[0, 0]
    extents = element_size[0, 0]
    elements = mass_density.shape[0]
    distinct = 7 * 64 * elements
    high_count = distinct // 128
    tables, node_weight = derivative_tables()
    velocity = moment / mass_density[None]
    pressure = jnp.exp(GAMMA * jnp.log(mass_density))
    scales = 2.0 / extents
    residual = jnp.zeros((4, elements, 512), jnp.float32)
    for axis_num in range(3):
        mom_flux = moment * velocity[axis_num][None]
        mom_flux = mom_flux.at[axis_num].add(pressure)
        fluxes = (
            jnp.concatenate([moment[axis_num][None], mom_flux], axis=0)
            * scales[axis_num][None, :, None]
        )
        change = jnp.dot(
            fluxes.reshape(4 * elements, 512), tables[axis_num], precision=lax.Precision.HIGHEST
        )
        residual = residual - change.reshape(4, elements, 512)
    jacobian = extents[0] * extents[1] * extents[2] / 8.0
    weight = jacobian[:, None] * node_weight[None]
    values = jnp.concatenate([residual * weight[None], weight[None]], axis=0).reshape(
        5, elements, 8, 64
    )
    last_face = jnp.roll(values[:, :, 7], 1, axis=1)
    first_face = values[:, :, 0] + last_face
    slabs = jnp.concatenate([first_face[:, :, None], values[:, :, 1:7]], axis=2)
    sums = slabs.reshape(5, high_count, 128)
    table = jnp.moveaxis(sums, 0, 1)
    section_ids = section_slots[0, 0]
    cross_ids = cross_slots[0, 0]
    section_send = pick_rows(table, section_ids, section_counts[0, 0])
    cross_send = pick_rows(table, cross_ids, cross_counts[0, 0])
    sections = lax.axis_size("cube").bit_length() - 1
    received = []
    gathered = lax.all_gather(section_send[None], "cube", axis=0, tiled=True)
    position = lax.axis_index("cube")
    for b in range(sections):
        partner = jnp.bitwise_xor(position, 1 << b)
        partner_block = lax.dynamic_index_in_dim(gathered, partner, 0, keepdims=False)
        received.append(partner_block[:, b])
    section_recv = jnp.stack(received, axis=1)
    padded = with_halo(cross_send, (("grp", 1),), 1)
    cross_recv = jnp.stack([padded[:, 0], padded[:, 3]], axis=1)
    table = add_rows(table, section_ids, section_recv)
    table = add_rows(table, cross_ids, cross_recv)
    totals = jnp.moveaxis(table, 0, 1)
    assembled = (totals[:4] / totals[4:]).reshape(4, elements, 7, 64)
    next_face = jnp.roll(assembled[:, :, 0], -1, axis=1)
    at_nodes = jnp.concatenate([assembled, next_face[:, :, None]], axis=2).reshape(4, elements, 512)
    new_density = mass_density + DT * at_nodes[0]
    new_momentum = moment + DT * at_nodes[1:]
    return (new_density[None, None], new_momentum[None, None])


def solution(mesh):
    placed = (
        P("grp", "cube", None, None),
        P("grp", "cube", None, None, None),
        P("grp", "cube", None, None),
        P("grp", "cube", None, None),
        P("grp", "cube", None),
        P("grp", "cube", None, None),
        P("grp", "cube", None),
    )
    return jax.shard_map(
        local,
        mesh=mesh,
        in_specs=placed,
        out_specs=(P("grp", "cube", None, None), P("grp", "cube", None, None, None)),
        check_vma=False,
    )
```

profile of v0, /device:TPU:1, one launch (start us, length us, event | category | flops | bytes accessed | tf_op | source)
XLA Modules:
  0.0 140.9 jit_solution(12547658558142981243)
XLA Ops:
  7.2 0.7 broadcast_divide_fusion
  8.0 0.7 multiply_bitcast_fusion.1
  8.7 1.1 slice_bitcast_fusion.5
  9.8 1.1 bitcast_divide_fusion
  10.9 0.8 broadcast_multiply_fusion.3
  12.1 1.1 convolution_subtract_fusion.2
  13.2 1.1 convolution_subtract_fusion.1
  14.3 1.1 fusion.25
  17.2 24.8 %while.51 = (s32[]{:T(128)}, f32[5,5,1024]{2,0,1:T(8,128)}, s32[5,1024]{1,0:T(8,128)S(1)}, f32[224,640]{1,0:T(8,128)S(1)}, s32[5]{0:T(128)S(1)}, /*index=5*/s32[]{:T(128)}, s32[]{:T(128)}) while((s32[]{:T(128)}, f32[5,5,1024]{2,0,1:T(8,128)}, s32[5,1024]{1,0:T(8,128)S(1)}, f32[224,640]{1,0:T(8,128)S(1)}, s32[5]{0:T(128)S(1)}, ...), condition=%wide.region_2.0_spmd, body=%wide.region_0.2_spmd.sunk | while | flops 1763431424 | bytes 7045221 | solution.py:107
  17.2 1.4 %fusion.65 = f32[1024,640]{0,1:T(8,128)S(1)} fusion(f32[224,640]{1,0:T(8,128)S(1)} %get-tuple-element.535, s32[1024]{0:T(1024)S(1)} %get-tuple-element.497), kind=kOutput, calls=%fused_computation.2.clone.1 | convolution fusion | flops 1761837056 | bytes 3198976 | tf_op jit(solution)/shard_map/while/body/eval_jaxpr/dot_general | solution.py:100
  19.1 0.7 dynamic_slice.95
  19.8 0.7 fusion.67
  20.5 1.7 %dynamic_update_slice.17 = f32[5,5,1024]{2,0,1:T(8,128)} dynamic-update-slice(f32[5,5,1024]{2,0,1:T(8,128)} %get-tuple-element.526, f32[1,5,1024]{2,0,1:T(1,128)S(1)} %copy.62, s32[]{:T(128)} %get-tuple-element.525, s32[]{:T(128)} %constant.335.clone.1..sunk, s32[]{:T(128)} %constant.335.clone.1..sunk) | dynamic-update-slice | bytes 40964 | tf_op jit(solution)/shard_map/while/body/jit(dynamic_update_index_in_dim)/dynamic_update_slice | solution.py:107
  22.2 1.5 %fusion.65 = f32[1024,640]{0,1:T(8,128)S(1)} fusion(f32[224,640]{1,0:T(8,128)S(1)} %get-tuple-element.535, s32[1024]{0:T(1024)S(1)} %get-tuple-element.497), kind=kOutput, calls=%fused_computation.2.clone.1 | convolution fusion | flops 1761837056 | bytes 3198976 | tf_op jit(solution)/shard_map/while/body/eval_jaxpr/dot_general | solution.py:100
  24.1 0.7 dynamic_slice.95
  24.7 0.7 fusion.67
  25.5 1.7 %dynamic_update_slice.17 = f32[5,5,1024]{2,0,1:T(8,128)} dynamic-update-slice(f32[5,5,1024]{2,0,1:T(8,128)} %get-tuple-element.526, f32[1,5,1024]{2,0,1:T(1,128)S(1)} %copy.62, s32[]{:T(128)} %get-tuple-element.525, s32[]{:T(128)} %constant.335.clone.1..sunk, s32[]{:T(128)} %constant.335.clone.1..sunk) | dynamic-update-slice | bytes 40964 | tf_op jit(solution)/shard_map/while/body/jit(dynamic_update_index_in_dim)/dynamic_update_slice | solution.py:107
  27.1 1.4 %fusion.65 = f32[1024,640]{0,1:T(8,128)S(1)} fusion(f32[224,640]{1,0:T(8,128)S(1)} %get-tuple-element.535, s32[1024]{0:T(1024)S(1)} %get-tuple-element.497), kind=kOutput, calls=%fused_computation.2.clone.1 | convolution fusion | flops 1761837056 | bytes 3198976 | tf_op jit(solution)/shard_map/while/body/eval_jaxpr/dot_general | solution.py:100
  29.0 0.7 dynamic_slice.95
  29.7 0.7 fusion.67
  30.4 1.7 %dynamic_update_slice.17 = f32[5,5,1024]{2,0,1:T(8,128)} dynamic-update-slice(f32[5,5,1024]{2,0,1:T(8,128)} %get-tuple-element.526, f32[1,5,1024]{2,0,1:T(1,128)S(1)} %copy.62, s32[]{:T(128)} %get-tuple-element.525, s32[]{:T(128)} %constant.335.clone.1..sunk, s32[]{:T(128)} %constant.335.clone.1..sunk) | dynamic-update-slice | bytes 40964 | tf_op jit(solution)/shard_map/while/body/jit(dynamic_update_index_in_dim)/dynamic_update_slice | solution.py:107
  32.1 1.5 %fusion.65 = f32[1024,640]{0,1:T(8,128)S(1)} fusion(f32[224,640]{1,0:T(8,128)S(1)} %get-tuple-element.535, s32[1024]{0:T(1024)S(1)} %get-tuple-element.497), kind=kOutput, calls=%fused_computation.2.clone.1 | convolution fusion | flops 1761837056 | bytes 3198976 | tf_op jit(solution)/shard_map/while/body/eval_jaxpr/dot_general | solution.py:100
  34.0 0.7 dynamic_slice.95
  34.6 0.7 fusion.67
  35.4 1.7 %dynamic_update_slice.17 = f32[5,5,1024]{2,0,1:T(8,128)} dynamic-update-slice(f32[5,5,1024]{2,0,1:T(8,128)} %get-tuple-element.526, f32[1,5,1024]{2,0,1:T(1,128)S(1)} %copy.62, s32[]{:T(128)} %get-tuple-element.525, s32[]{:T(128)} %constant.335.clone.1..sunk, s32[]{:T(128)} %constant.335.clone.1..sunk) | dynamic-update-slice | bytes 40964 | tf_op jit(solution)/shard_map/while/body/jit(dynamic_update_index_in_dim)/dynamic_update_slice | solution.py:107
  37.1 1.4 %fusion.65 = f32[1024,640]{0,1:T(8,128)S(1)} fusion(f32[224,640]{1,0:T(8,128)S(1)} %get-tuple-element.535, s32[1024]{0:T(1024)S(1)} %get-tuple-element.497), kind=kOutput, calls=%fused_computation.2.clone.1 | convolution fusion | flops 1761837056 | bytes 3198976 | tf_op jit(solution)/shard_map/while/body/eval_jaxpr/dot_general | solution.py:100
  38.9 0.7 dynamic_slice.95
  39.6 0.7 fusion.67
  40.3 1.7 %dynamic_update_slice.17 = f32[5,5,1024]{2,0,1:T(8,128)} dynamic-update-slice(f32[5,5,1024]{2,0,1:T(8,128)} %get-tuple-element.526, f32[1,5,1024]{2,0,1:T(1,128)S(1)} %copy.62, s32[]{:T(128)} %get-tuple-element.525, s32[]{:T(128)} %constant.335.clone.1..sunk, s32[]{:T(128)} %constant.335.clone.1..sunk) | dynamic-update-slice | bytes 40964 | tf_op jit(solution)/shard_map/while/body/jit(dynamic_update_index_in_dim)/dynamic_update_slice | solution.py:107
  42.0 6.4 %while.53 = (s32[]{:T(128)}, f32[2,5,1024]{2,1,0:T(8,128)S(1)}, s32[2,1024]{1,0:T(2,128)S(1)}, f32[224,640]{1,0:T(8,128)S(1)}, s32[2]{0:T(128)S(1)}, /*index=5*/s32[]{:T(128)}) while((s32[]{:T(128)}, f32[2,5,1024]{2,1,0:T(8,128)S(1)}, s32[2,1024]{1,0:T(2,128)S(1)}, f32[224,640]{1,0:T(8,128)S(1)}, s32[2]{0:T(128)S(1)}, ...), condition=%wide.region_7.8_spmd, body=%wide.region_5.7_spmd.sunk | while | flops 1763431424 | bytes 6987869 | solution.py:107
  42.1 1.5 %fusion.72 = f32[1024,640]{0,1:T(8,128)S(1)} fusion(f32[224,640]{1,0:T(8,128)S(1)} %get-tuple-element.569, s32[1024]{0:T(1024)S(1)} %get-tuple-element.510), kind=kOutput, calls=%fused_computation.37.clone.1 | convolution fusion | flops 1761837056 | bytes 3198976 | tf_op jit(solution)/shard_map/while/body/eval_jaxpr/dot_general | solution.py:100
  45.3 1.4 %fusion.72 = f32[1024,640]{0,1:T(8,128)S(1)} fusion(f32[224,640]{1,0:T(8,128)S(1)} %get-tuple-element.569, s32[1024]{0:T(1024)S(1)} %get-tuple-element.510), kind=kOutput, calls=%fused_computation.37.clone.1 | convolution fusion | flops 1761837056 | bytes 3198976 | tf_op jit(solution)/shard_map/while/body/eval_jaxpr/dot_general | solution.py:100
  48.4 4.4 %collective-permute-start = (f32[5,1,1024]{2,0,1:T(8,128)S(1)}, f32[5,1,1024]{2,0,1:T(8,128)S(1)}, u32[]{:S(2)}, u32[]{:S(2)}) collective-permute-start(f32[5,1,1024]{2,0,1:T(8,128)S(1)} %get-tuple-element.381), channel_id=1, source_target_pairs={{0,32},{32,64},{64,96},{96,128},{128,160},{160,192},{192,224},{224... | collective-permute-start | bytes 61448 | tf_op jit(solution)/shard_map/ppermute | solution.py:19
  52.8 9.7 %collective-permute-start.1 = (f32[5,1,1024]{2,0,1:T(8,128)S(1)}, f32[5,1,1024]{2,0,1:T(8,128)S(1)}, u32[]{:S(2)}, u32[]{:S(2)}) collective-permute-start(f32[5,1,1024]{2,0,1:T(8,128)S(1)} %get-tuple-element.382), channel_id=1, source_target_pairs={{32,0},{64,32},{96,64},{128,96},{160,128},{192,160},{224,192},{256... | collective-permute-start | bytes 61448 | tf_op jit(solution)/shard_map/ppermute | solution.py:21
  62.5 0.8 collective-permute-done.1
  63.3 47.1 %all-gather.3.cloned.1.call-done = f32[160,5,1024]{2,1,0:T(8,128)} async-done(((f32[5,5,1024]{2,1,0:T(8,128)}), f32[160,5,1024]{2,1,0:T(8,128)}) %all-gather.3.cloned.1.call-update) | async-done | bytes 3276816 | tf_op jit(solution)/shard_map/all_gather | solution.py:169
  110.4 1.3 constant_dynamic-slice_fusion.4
  112.2 13.4 %while.52 = (s32[]{:T(128)}, f32[224,640]{1,0:T(8,128)S(1)}, s32[5,1024]{1,0:T(8,128)S(1)}, f32[5,5,1024]{2,1,0:T(8,128)S(1)}, s32[]{:T(128)}) while((s32[]{:T(128)}, f32[224,640]{1,0:T(8,128)S(1)}, s32[5,1024]{1,0:T(8,128)S(1)}, f32[5,5,1024]{2,1,0:T(8,128)S(1)}, s32[]{:T(128)}) %tuple.161), condition=%wide.region_4.5_spmd, body=%wide.region_3.4_spmd.sunk | while | flops 1763146752 | bytes 7528517 | solution.py:122
  112.6 2.2 %convolution_add_fusion.4 = f32[224,640]{1,0:T(8,128)S(1)} fusion(f32[224,640]{1,0:T(8,128)S(1)} %get-tuple-element.545, f32[1024,640]{0,1:T(8,128)S(1)} %bitcast.147, s32[1024]{0:T(1024)S(1)} %get-tuple-element.504), kind=kOutput, calls=%fused_computation.19.clone.1 | convolution fusion | flops 1762209792 | bytes 3772416 | tf_op jit(solution)/shard_map/while/body/eval_jaxpr/dot_general | solution.py:117
  115.3 2.2 %convolution_add_fusion.4 = f32[224,640]{1,0:T(8,128)S(1)} fusion(f32[224,640]{1,0:T(8,128)S(1)} %get-tuple-element.545, f32[1024,640]{0,1:T(8,128)S(1)} %bitcast.147, s32[1024]{0:T(1024)S(1)} %get-tuple-element.504), kind=kOutput, calls=%fused_computation.19.clone.1 | convolution fusion | flops 1762209792 | bytes 3772416 | tf_op jit(solution)/shard_map/while/body/eval_jaxpr/dot_general | solution.py:117
  118.0 2.2 %convolution_add_fusion.4 = f32[224,640]{1,0:T(8,128)S(1)} fusion(f32[224,640]{1,0:T(8,128)S(1)} %get-tuple-element.545, f32[1024,640]{0,1:T(8,128)S(1)} %bitcast.147, s32[1024]{0:T(1024)S(1)} %get-tuple-element.504), kind=kOutput, calls=%fused_computation.19.clone.1 | convolution fusion | flops 1762209792 | bytes 3772416 | tf_op jit(solution)/shard_map/while/body/eval_jaxpr/dot_general | solution.py:117
  120.7 2.2 %convolution_add_fusion.4 = f32[224,640]{1,0:T(8,128)S(1)} fusion(f32[224,640]{1,0:T(8,128)S(1)} %get-tuple-element.545, f32[1024,640]{0,1:T(8,128)S(1)} %bitcast.147, s32[1024]{0:T(1024)S(1)} %get-tuple-element.504), kind=kOutput, calls=%fused_computation.19.clone.1 | convolution fusion | flops 1762209792 | bytes 3772416 | tf_op jit(solution)/shard_map/while/body/eval_jaxpr/dot_general | solution.py:117
  123.3 2.2 %convolution_add_fusion.4 = f32[224,640]{1,0:T(8,128)S(1)} fusion(f32[224,640]{1,0:T(8,128)S(1)} %get-tuple-element.545, f32[1024,640]{0,1:T(8,128)S(1)} %bitcast.147, s32[1024]{0:T(1024)S(1)} %get-tuple-element.504), kind=kOutput, calls=%fused_computation.19.clone.1 | convolution fusion | flops 1762209792 | bytes 3772416 | tf_op jit(solution)/shard_map/while/body/eval_jaxpr/dot_general | solution.py:117
  125.6 5.4 %while.54 = (s32[]{:T(128)}, f32[224,640]{1,0:T(8,128)S(1)}, s32[2,1024]{1,0:T(2,128)S(1)}, f32[2,5,1024]{2,1,0:T(8,128)S(1)}, s32[]{:T(128)}) while((s32[]{:T(128)}, f32[224,640]{1,0:T(8,128)S(1)}, s32[2,1024]{1,0:T(2,128)S(1)}, f32[2,5,1024]{2,1,0:T(8,128)S(1)}, s32[]{:T(128)}) %tuple.159), condition=%wide.region_9.10_spmd, body=%wide.region_8.9_spmd.sunk | while | flops 1763146752 | bytes 7528517 | solution.py:122
  126.0 2.2 %convolution_add_fusion.5 = f32[224,640]{1,0:T(8,128)S(1)} fusion(f32[224,640]{1,0:T(8,128)S(1)} %get-tuple-element.578, f32[1024,640]{0,1:T(8,128)S(1)} %bitcast.148, s32[1024]{0:T(1024)S(1)} %get-tuple-element.517), kind=kOutput, calls=%fused_computation.54.clone.1 | convolution fusion | flops 1762209792 | bytes 3772416 | tf_op jit(solution)/shard_map/while/body/eval_jaxpr/dot_general | solution.py:117
  128.7 2.2 %convolution_add_fusion.5 = f32[224,640]{1,0:T(8,128)S(1)} fusion(f32[224,640]{1,0:T(8,128)S(1)} %get-tuple-element.578, f32[1024,640]{0,1:T(8,128)S(1)} %bitcast.148, s32[1024]{0:T(1024)S(1)} %get-tuple-element.517), kind=kOutput, calls=%fused_computation.54.clone.1 | convolution fusion | flops 1762209792 | bytes 3772416 | tf_op jit(solution)/shard_map/while/body/eval_jaxpr/dot_general | solution.py:117
  132.5 0.8 add.181
  133.4 0.7 add.180
  (142 shorter events, 12.3 us)
Async XLA Ops:
  7.2 4.6 %copy-start = (f32[1,1,3,64,512]{4,3,2,1,0:T(8,128)S(1)}, f32[1,1,3,64,512]{4,3,2,1,0:T(8,128)}, u32[]{:S(2)}) copy-start(f32[1,1,3,64,512]{4,3,2,1,0:T(8,128)} %param.26) | copy-start | bytes 1179652
  7.2 4.8 %copy-start.1 = (f32[1,1,64,512]{3,2,1,0:T(8,128)S(1)}, f32[1,1,64,512]{3,2,1,0:T(8,128)}, u32[]{:S(2)}) copy-start(f32[1,1,64,512]{3,2,1,0:T(8,128)} %param.25) | copy-start | bytes 393220
  7.2 103.2 %all-gather.3.cloned.1.call-start = ((), (), s32[]{:S(2)}) async-start(), calls=%async_computation | async-start | bytes 5406720 | tf_op jit(solution)/shard_map/all_gather | solution.py:169
  8.7 3.4 %copy-start.2 = (f32[512,512,1]{1,0,2:T(8,128)S(1)}, f32[512,512,1]{1,0,2:T(8,128)}, u32[]{:S(2)}) copy-start(f32[512,512,1]{1,0,2:T(8,128)} %constant.360) | copy-start | bytes 3145732
  10.9 2.3 %copy-start.4 = (f32[512,512,1]{1,0,2:T(8,128)S(1)}, f32[512,512,1]{1,0,2:T(8,128)}, u32[]{:S(2)}) copy-start(f32[512,512,1]{1,0,2:T(8,128)} %constant.361) | copy-start | bytes 3145732
  12.0 2.3 %copy-start.3 = (f32[512,512,1]{1,0,2:T(8,128)S(1)}, f32[512,512,1]{1,0,2:T(8,128)}, u32[]{:S(2)}) copy-start(f32[512,512,1]{1,0,2:T(8,128)} %constant.362) | copy-start | bytes 3145732
  14.3 1.3 copy-start.7
  16.3 0.8 copy-start.6
  16.4 0.8 copy-start.8
  17.1 24.9 %copy-start.5 = (s32[1,1,2,1024]{3,2,1,0:T(2,128)S(1)}, s32[1,1,2,1024]{3,2,1,0:T(2,128)}, u32[]{:S(2)}) copy-start(s32[1,1,2,1024]{3,2,1,0:T(2,128)} %param.30) | copy-start | bytes 24580
  17.2 24.9 %copy-start.9 = (s32[1,1,2]{2,1,0:T(1,128)S(1)}, s32[1,1,2]{2,1,0:T(1,128)}, u32[]{:S(2)}) copy-start(s32[1,1,2]{2,1,0:T(1,128)} %param.31) | copy-start | bytes 28
  48.4 14.1 %collective-permute-start = (f32[5,1,1024]{2,0,1:T(8,128)S(1)}, f32[5,1,1024]{2,0,1:T(8,128)S(1)}, u32[]{:S(2)}, u32[]{:S(2)}) collective-permute-start(f32[5,1,1024]{2,0,1:T(8,128)S(1)} %get-tuple-element.381), channel_id=1, source_target_pairs={{0,32},{32,64},{64,96},{96,128},{128,160},{160,192},{192,224},{224... | collective-permute-start | bytes 61448 | tf_op jit(solution)/shard_map/ppermute | solution.py:19
  52.8 10.5 %collective-permute-start.1 = (f32[5,1,1024]{2,0,1:T(8,128)S(1)}, f32[5,1,1024]{2,0,1:T(8,128)S(1)}, u32[]{:S(2)}, u32[]{:S(2)}) collective-permute-start(f32[5,1,1024]{2,0,1:T(8,128)S(1)} %get-tuple-element.382), channel_id=1, source_target_pairs={{32,0},{64,32},{96,64},{128,96},{160,128},{192,160},{224,192},{256... | collective-permute-start | bytes 61448 | tf_op jit(solution)/shard_map/ppermute | solution.py:21
Sparse Core Ops, SparseCore 0:
  42.1 68.2 all-gather.2
where the time goes:
time: 141 us
  waiting for transfers between devices  47.9 us (34%)
  matrix products  29 us (21%)
  local copies, waits for them, and re-layouts  18.1 us (13%)
  other arithmetic  16.4 us (12%)
  between operations  14.6 us (10%)
  starting transfers between devices  14.1 us (10%)
    all_gather x1, waiting for transfers between devices, local(): gathered = lax.all_gather(section_send[None], 'cube', axis=0, tiled=True)  47.1 us
    dot_general x7, matrix products, add_one_row(): lax.dot_general(high_part, spread, (((0,), (0,)), ((), ())), precision=la...  15.6 us
    dot_general x7, matrix products, pick_one_row(): jnp.dot(high_part, flat_table, precision=lax.Precision.HIGHEST)  10.1 us
    ppermute x1, starting transfers between devices, with_halo(): lax.ppermute(head, axis, [((i + 1) % count, i) for i in range(count)])  9.68 us
    dynamic_update_slice x10, local copies, waits for them, and re-layouts, pick_rows(): return jnp.moveaxis(lax.map(pick_one_row, (slot_ids, counts)), 0, 1)  8.4 us
    convert_element_type x7, other arithmetic, pick_one_row(): live_mask = (jnp.arange(row_ids.shape[0]) < count).astype(jnp.float32)  4.62 us
    dynamic_slice x21, local copies, waits for them, and re-layouts, pick_rows(): return jnp.moveaxis(lax.map(pick_one_row, (slot_ids, counts)), 0, 1)  4.58 us
    ppermute x1, starting transfers between devices, with_halo(): lax.ppermute(tail, axis, [(i, (i + 1) % count) for i in range(count)])  4.35 us
  transfers between devices with their start and end apart: 3, of which 2 were waited for; matrix products, arithmetic and copies ran while one was open for 4% of the time, Pallas kernels for 0%

commit v1 on v0

--- a/solution.py
+++ b/solution.py
@@ -166,7 +166,9 @@
     cross_send = pick_rows(table, cross_ids, cross_counts[0, 0])
     sections = lax.axis_size("cube").bit_length() - 1
     received = []
-    gathered = lax.all_gather(section_send[None], "cube", axis=0, tiled=True)
+    block = section_send[None]
+    outgoing = jnp.stack([block] * lax.axis_size("cube"))
+    gathered = jnp.concatenate(lax.all_to_all(outgoing, "cube", 0, 0), axis=0)
     position = lax.axis_index("cube")
     for b in range(sections):
         partner = jnp.bitwise_xor(position, 1 << b)

time: 141 us -> 106 us (0.75)
  waiting for transfers between devices: 47.9 us -> 23.8 us
  between operations: 14.6 us -> 1.2 us
  starting transfers between devices: 14.1 us -> 22 us
  local copies, waits for them, and re-layouts: 18.1 us -> 12.9 us
    all_gather x1 -> x0, waiting for transfers between devices: 47.1 us -> none  [local(): gathered = lax.all_gather(section_send[None], 'cube', axis=0, tiled=True)]
    all_to_all x0 -> x1, waiting for transfers between devices: none -> 23 us  [local(): gathered = jnp.concatenate(lax.all_to_all(outgoing, 'cube', 0, 0), axis=0)]
    all_to_all x0 -> x1, starting transfers between devices: none -> 11.4 us  [local(): gathered = jnp.concatenate(lax.all_to_all(outgoing, 'cube', 0, 0), axis=0)]
    dynamic_update_slice x10 -> x0, local copies, waits for them, and re-layouts: 8.4 us -> none  [pick_rows(): return jnp.moveaxis(lax.map(pick_one_row, (slot_ids, counts)), 0, 1)]
    another operation x0 -> x1, local copies, waits for them, and re-layouts: none -> 3.41 us  [local(): outgoing = jnp.stack([block] * lax.axis_size('cube'))]
    ppermute x1, starting transfers between devices: 4.35 us -> 1.92 us  [with_halo(): lax.ppermute(tail, axis, [(i, (i + 1) % count) for i in range(count)])]
  transfers between devices with their start and end apart: 3 -> 3, of which waited for: 2 -> 2; matrix products, arithmetic and copies ran while one was open for 4% -> 6% of each run, Pallas kernels for 0% -> 0%
where the time goes in v1:
time: 106 us
  matrix products  29.1 us (27%)
  waiting for transfers between devices  23.8 us (22%)
  starting transfers between devices  22 us (21%)
  other arithmetic  15.9 us (15%)
  local copies, waits for them, and re-layouts  12.9 us (12%)
  between operations  1.2 us (1%)
    all_to_all x1, waiting for transfers between devices, local(): gathered = jnp.concatenate(lax.all_to_all(outgoing, 'cube', 0, 0), axis=0)  23 us
    dot_general x7, matrix products, add_one_row(): lax.dot_general(high_part, spread, (((0,), (0,)), ((), ())), precision=la...  15.7 us
    all_to_all x1, starting transfers between devices, local(): gathered = jnp.concatenate(lax.all_to_all(outgoing, 'cube', 0, 0), axis=0)  11.4 us
    dot_general x7, matrix products, pick_one_row(): jnp.dot(high_part, flat_table, precision=lax.Precision.HIGHEST)  10.2 us
    ppermute x1, starting transfers between devices, with_halo(): lax.ppermute(head, axis, [((i + 1) % count, i) for i in range(count)])  8.67 us
    dynamic_slice x21, local copies, waits for them, and re-layouts, pick_rows(): return jnp.moveaxis(lax.map(pick_one_row, (slot_ids, counts)), 0, 1)  4.39 us
    convert_element_type x7, other arithmetic, pick_one_row(): live_mask = (jnp.arange(row_ids.shape[0]) < count).astype(jnp.float32)  4.1 us
    another operation x1, local copies, waits for them, and re-layouts, local(): outgoing = jnp.stack([block] * lax.axis_size('cube'))  3.41 us
  transfers between devices with their start and end apart: 3, of which 2 were waited for; matrix products, arithmetic and copies ran while one was open for 6% of the time, Pallas kernels for 0%

profile of v1, /device:TPU:1, one launch (start us, length us, event | category | flops | bytes accessed | tf_op | source)
XLA Modules:
  0.0 105.9 jit_solution(17025882488996564671)
XLA Ops:
  0.7 0.7 broadcast_divide_fusion
  1.4 0.7 multiply_bitcast_fusion
  2.1 1.1 %slice_bitcast_fusion.5 = (f32[1,64,512]{2,1,0:T(8,128)S(1)}, f32[1,64,512]{2,1,0:T(8,128)S(1)}, f32[1,64,512]{2,1,0:T(8,128)S(1)}) fusion(f32[1,1,3,64,512]{4,3,2,1,0:T(8,128)} %param.26), kind=kLoop, calls=%fused_computation.119 | loop fusion | bytes 786432 | tf_op jit(solution)/shard_map/slice | solution.py:146
  3.2 1.1 %bitcast_divide_fusion = f32[3,64,512]{2,1,0:T(8,128)S(1)} fusion(f32[1,1,3,64,512]{4,3,2,1,0:T(8,128)} %param.26, f32[64,512]{1,0:T(8,128)} %bitcast.156), kind=kLoop, calls=%fused_computation.93 | loop fusion | flops 98304 | bytes 917504 | tf_op jit(solution)/shard_map/div | solution.py:138
  4.4 0.8 broadcast_multiply_fusion.3
  5.5 1.1 %convolution_subtract_fusion.2 = f32[4,64,512]{2,1,0:T(8,128)S(1)} fusion(f32[512,512,1]{1,0,2:T(8,128)S(1)} %copy-done.2, f32[3,64,512]{2,1,0:T(8,128)S(1)} %get-tuple-element.394, f32[1,64,512]{2,1,0:T(8,128)S(1)} %get-tuple-element.385, f32[64]{0:T(128)S(1)} %get-tuple-element.399), kind=kOutput, calls=%fused_computation.76 | convolution fusion | flops 805699584 | bytes 2097408 | tf_op jit(solution)/shard_map/dot_general | solution.py:149
  6.6 1.1 %convolution_subtract_fusion.1 = f32[4,64,512]{2,1,0:T(8,128)S(1)} fusion(f32[4,64,512]{2,1,0:T(8,128)S(1)} %convolution_subtract_fusion.2, f32[512,512,1]{1,0,2:T(8,128)S(1)} %copy-done.4, f32[3,64,512]{2,1,0:T(8,128)S(1)} %get-tuple-element.393, f32[1,64,512]{2,1,0:T(8,128)S(1)} %get-tuple-element.384, f32[64]{0:T(128)S(1)} %get-tuple-element.398), kind=kOutput, calls=%fused_computation.75 | convolution fusion | flops 805699584 | bytes 2621696 | tf_op jit(solution)/shard_map/dot_general | solution.py:149
  7.8 1.1 %fusion.25 = f32[4,64,512]{2,1,0:T(8,128)S(1)} fusion(f32[4,64,512]{2,1,0:T(8,128)S(1)} %convolution_subtract_fusion.1, f32[512,512,1]{1,0,2:T(8,128)S(1)} %copy-done.3, f32[3,64,512]{2,1,0:T(8,128)S(1)} %get-tuple-element.392, f32[1,64,512]{2,1,0:T(8,128)S(1)} %get-tuple-element.383, f32[64,512]{1,0:T(8,128)S(1)} %broadcast_multiply_fusion.3, ...), kind=kOutput, calls=%fused_computation.77 | convolution fusion | flops 805830656 | bytes 2752768 | tf_op jit(solution)/shard_map/dot_general | solution.py:149
  10.6 15.7 %while.51 = (s32[]{:T(128)}, f32[5,5,1024]{2,1,0:T(8,128)S(1)}, s32[5,1024]{1,0:T(8,128)S(1)}, f32[224,640]{1,0:T(8,128)S(1)}, s32[5]{0:T(128)S(1)}, /*index=5*/s32[]{:T(128)}) while((s32[]{:T(128)}, f32[5,5,1024]{2,1,0:T(8,128)S(1)}, s32[5,1024]{1,0:T(8,128)S(1)}, f32[224,640]{1,0:T(8,128)S(1)}, s32[5]{0:T(128)S(1)}, ...), condition=%wide.region_2.0_spmd, body=%wide.region_0.2_spmd.sunk | while | flops 1763431424 | bytes 6987869 | solution.py:107
  10.6 1.5 %fusion.65 = f32[1024,640]{0,1:T(8,128)S(1)} fusion(f32[224,640]{1,0:T(8,128)S(1)} %get-tuple-element.547, s32[1024]{0:T(1024)S(1)} %get-tuple-element.511), kind=kOutput, calls=%fused_computation.2.clone.1 | convolution fusion | flops 1761837056 | bytes 3198976 | tf_op jit(solution)/shard_map/while/body/eval_jaxpr/dot_general | solution.py:100
  12.5 0.6 dynamic_slice.95
  13.1 0.6 fusion.67
  13.8 1.5 %fusion.65 = f32[1024,640]{0,1:T(8,128)S(1)} fusion(f32[224,640]{1,0:T(8,128)S(1)} %get-tuple-element.547, s32[1024]{0:T(1024)S(1)} %get-tuple-element.511), kind=kOutput, calls=%fused_computation.2.clone.1 | convolution fusion | flops 1761837056 | bytes 3198976 | tf_op jit(solution)/shard_map/while/body/eval_jaxpr/dot_general | solution.py:100
  15.7 0.6 dynamic_slice.95
  16.3 0.6 fusion.67
  16.9 1.4 %fusion.65 = f32[1024,640]{0,1:T(8,128)S(1)} fusion(f32[224,640]{1,0:T(8,128)S(1)} %get-tuple-element.547, s32[1024]{0:T(1024)S(1)} %get-tuple-element.511), kind=kOutput, calls=%fused_computation.2.clone.1 | convolution fusion | flops 1761837056 | bytes 3198976 | tf_op jit(solution)/shard_map/while/body/eval_jaxpr/dot_general | solution.py:100
  18.8 0.6 dynamic_slice.95
  19.4 0.6 fusion.67
  20.1 1.5 %fusion.65 = f32[1024,640]{0,1:T(8,128)S(1)} fusion(f32[224,640]{1,0:T(8,128)S(1)} %get-tuple-element.547, s32[1024]{0:T(1024)S(1)} %get-tuple-element.511), kind=kOutput, calls=%fused_computation.2.clone.1 | convolution fusion | flops 1761837056 | bytes 3198976 | tf_op jit(solution)/shard_map/while/body/eval_jaxpr/dot_general | solution.py:100
  22.0 0.6 dynamic_slice.95
  22.6 0.6 fusion.67
  23.2 1.5 %fusion.65 = f32[1024,640]{0,1:T(8,128)S(1)} fusion(f32[224,640]{1,0:T(8,128)S(1)} %get-tuple-element.547, s32[1024]{0:T(1024)S(1)} %get-tuple-element.511), kind=kOutput, calls=%fused_computation.2.clone.1 | convolution fusion | flops 1761837056 | bytes 3198976 | tf_op jit(solution)/shard_map/while/body/eval_jaxpr/dot_general | solution.py:100
  25.1 0.6 dynamic_slice.95
  26.4 3.4 %stack.9 = f32[32,1,5,5,1024]{4,1,3,2,0:T(1,128)} broadcast(f32[5,5,1024]{2,1,0:T(8,128)S(1)} %copy.40), dimensions={2,3,4} | broadcast | bytes 3379200 | tf_op jit(solution)/shard_map/stack | solution.py:170
  29.8 11.4 %all-to-all-start = ((f32[32,1,5,5,1024]{4,1,3,2,0:T(1,128)}), f32[32,1,5,5,1024]{4,1,3,2,0:T(1,128)}, u32[]{:S(2)}, u32[]{:S(2)}) async-start(f32[32,1,5,5,1024]{4,1,3,2,0:T(1,128)} %stack.9), calls=%async_computation | async-start | bytes 6553600 | tf_op jit(solution)/shard_map/all_to_all | solution.py:171
  41.2 6.5 %while.53 = (s32[]{:T(128)}, f32[2,5,1024]{2,1,0:T(8,128)S(1)}, s32[2,1024]{1,0:T(2,128)S(1)}, f32[224,640]{1,0:T(8,128)S(1)}, s32[2]{0:T(128)S(1)}, /*index=5*/s32[]{:T(128)}) while((s32[]{:T(128)}, f32[2,5,1024]{2,1,0:T(8,128)S(1)}, s32[2,1024]{1,0:T(2,128)S(1)}, f32[224,640]{1,0:T(8,128)S(1)}, s32[2]{0:T(128)S(1)}, ...), condition=%wide.region_7.8_spmd, body=%wide.region_5.7_spmd.sunk | while | flops 1763431424 | bytes 6987869 | solution.py:107
  41.3 1.5 %fusion.72 = f32[1024,640]{0,1:T(8,128)S(1)} fusion(f32[224,640]{1,0:T(8,128)S(1)} %get-tuple-element.580, s32[1024]{0:T(1024)S(1)} %get-tuple-element.524), kind=kOutput, calls=%fused_computation.38.clone.1 | convolution fusion | flops 1761837056 | bytes 3198976 | tf_op jit(solution)/shard_map/while/body/eval_jaxpr/dot_general | solution.py:100
  43.2 0.7 dynamic_slice.99
  43.8 0.6 fusion.74
  44.5 1.5 %fusion.72 = f32[1024,640]{0,1:T(8,128)S(1)} fusion(f32[224,640]{1,0:T(8,128)S(1)} %get-tuple-element.580, s32[1024]{0:T(1024)S(1)} %get-tuple-element.524), kind=kOutput, calls=%fused_computation.38.clone.1 | convolution fusion | flops 1761837056 | bytes 3198976 | tf_op jit(solution)/shard_map/while/body/eval_jaxpr/dot_general | solution.py:100
  46.4 0.7 dynamic_slice.99
  47.1 0.6 fusion.74
  47.7 1.9 %collective-permute-start = (f32[5,1,1024]{2,0,1:T(8,128)S(1)}, f32[5,1,1024]{2,0,1:T(8,128)S(1)}, u32[]{:S(2)}, u32[]{:S(2)}) collective-permute-start(f32[5,1,1024]{2,0,1:T(8,128)S(1)} %get-tuple-element.395), channel_id=1, source_target_pairs={{0,32},{32,64},{64,96},{96,128},{128,160},{160,192},{192,224},{224... | collective-permute-start | bytes 61448 | tf_op jit(solution)/shard_map/ppermute | solution.py:19
  49.7 8.7 %collective-permute-start.1 = (f32[5,1,1024]{2,0,1:T(8,128)S(1)}, f32[5,1,1024]{2,0,1:T(8,128)S(1)}, u32[]{:S(2)}, u32[]{:S(2)}) collective-permute-start(f32[5,1,1024]{2,0,1:T(8,128)S(1)} %get-tuple-element.396), channel_id=1, source_target_pairs={{32,0},{64,32},{96,64},{128,96},{160,128},{192,160},{224,192},{256... | collective-permute-start | bytes 61448 | tf_op jit(solution)/shard_map/ppermute | solution.py:21
  58.4 0.8 collective-permute-done.1
  59.2 23.0 %all-to-all-done = f32[32,1,5,5,1024]{4,1,3,2,0:T(1,128)} async-done(((f32[32,1,5,5,1024]{4,1,3,2,0:T(1,128)}), f32[32,1,5,5,1024]{4,1,3,2,0:T(1,128)}, u32[]{:S(2)}, u32[]{:S(2)}) %all-to-all-start) | async-done | bytes 3276832 | tf_op jit(solution)/shard_map/all_to_all | solution.py:171
  82.1 1.1 %constant_dynamic-slice_fusion.5 = (f32[1,1,5,5,1024]{4,1,3,2,0:T(1,128)S(1)}, f32[1,1,5,5,1024]{4,1,3,2,0:T(1,128)S(1)}, f32[1,1,5,5,1024]{4,1,3,2,0:T(1,128)S(...) fusion(f32[32,1,5,5,1024]{4,1,3,2,0:T(1,128)} %all-to-all-done, s32[]{:T(128)S(6)} %select_n.125, ...), kind=kLoop, calls=%fused_computation.127 | loop fusion | bytes 1024020 | tf_op jit(solution)/shard_map/jit(dynamic_index_in_dim)/dynamic_slice | solution.py:175
  83.8 13.6 %while.52 = (s32[]{:T(128)}, f32[224,640]{1,0:T(8,128)S(1)}, s32[5,1024]{1,0:T(8,128)S(1)}, f32[5,5,1024]{2,0,1:T(8,128)S(1)}, s32[]{:T(128)}) while((s32[]{:T(128)}, f32[224,640]{1,0:T(8,128)S(1)}, s32[5,1024]{1,0:T(8,128)S(1)}, f32[5,5,1024]{2,0,1:T(8,128)S(1)}, s32[]{:T(128)}) %tuple.162), condition=%wide.region_4.5_spmd, body=%wide.region_3.4_spmd.sunk | while | flops 1763146752 | bytes 7569477 | solution.py:122
  84.3 2.2 %convolution_add_fusion.4 = f32[224,640]{1,0:T(8,128)S(1)} fusion(f32[224,640]{1,0:T(8,128)S(1)} %get-tuple-element.556, f32[1024,640]{0,1:T(8,128)S(1)} %bitcast.147, s32[1024]{0:T(1024)S(1)} %get-tuple-element.518), kind=kOutput, calls=%fused_computation.19.clone.1 | convolution fusion | flops 1762209792 | bytes 3772416 | tf_op jit(solution)/shard_map/while/body/eval_jaxpr/dot_general | solution.py:117
  87.0 2.2 %convolution_add_fusion.4 = f32[224,640]{1,0:T(8,128)S(1)} fusion(f32[224,640]{1,0:T(8,128)S(1)} %get-tuple-element.556, f32[1024,640]{0,1:T(8,128)S(1)} %bitcast.147, s32[1024]{0:T(1024)S(1)} %get-tuple-element.518), kind=kOutput, calls=%fused_computation.19.clone.1 | convolution fusion | flops 1762209792 | bytes 3772416 | tf_op jit(solution)/shard_map/while/body/eval_jaxpr/dot_general | solution.py:117
  89.7 2.2 %convolution_add_fusion.4 = f32[224,640]{1,0:T(8,128)S(1)} fusion(f32[224,640]{1,0:T(8,128)S(1)} %get-tuple-element.556, f32[1024,640]{0,1:T(8,128)S(1)} %bitcast.147, s32[1024]{0:T(1024)S(1)} %get-tuple-element.518), kind=kOutput, calls=%fused_computation.19.clone.1 | convolution fusion | flops 1762209792 | bytes 3772416 | tf_op jit(solution)/shard_map/while/body/eval_jaxpr/dot_general | solution.py:117
  92.4 2.2 %convolution_add_fusion.4 = f32[224,640]{1,0:T(8,128)S(1)} fusion(f32[224,640]{1,0:T(8,128)S(1)} %get-tuple-element.556, f32[1024,640]{0,1:T(8,128)S(1)} %bitcast.147, s32[1024]{0:T(1024)S(1)} %get-tuple-element.518), kind=kOutput, calls=%fused_computation.19.clone.1 | convolution fusion | flops 1762209792 | bytes 3772416 | tf_op jit(solution)/shard_map/while/body/eval_jaxpr/dot_general | solution.py:117
  95.1 2.2 %convolution_add_fusion.4 = f32[224,640]{1,0:T(8,128)S(1)} fusion(f32[224,640]{1,0:T(8,128)S(1)} %get-tuple-element.556, f32[1024,640]{0,1:T(8,128)S(1)} %bitcast.147, s32[1024]{0:T(1024)S(1)} %get-tuple-element.518), kind=kOutput, calls=%fused_computation.19.clone.1 | convolution fusion | flops 1762209792 | bytes 3772416 | tf_op jit(solution)/shard_map/while/body/eval_jaxpr/dot_general | solution.py:117
  97.4 5.4 %while.54 = (s32[]{:T(128)}, f32[224,640]{1,0:T(8,128)S(1)}, s32[2,1024]{1,0:T(2,128)S(1)}, f32[2,5,1024]{2,1,0:T(8,128)S(1)}, s32[]{:T(128)}) while((s32[]{:T(128)}, f32[224,640]{1,0:T(8,128)S(1)}, s32[2,1024]{1,0:T(2,128)S(1)}, f32[2,5,1024]{2,1,0:T(8,128)S(1)}, s32[]{:T(128)}) %tuple.160), condition=%wide.region_9.10_spmd, body=%wide.region_8.9_spmd.sunk | while | flops 1763146752 | bytes 7528517 | solution.py:122
  97.8 2.2 %convolution_add_fusion.5 = f32[224,640]{1,0:T(8,128)S(1)} fusion(f32[224,640]{1,0:T(8,128)S(1)} %get-tuple-element.589, f32[1024,640]{0,1:T(8,128)S(1)} %bitcast.148, s32[1024]{0:T(1024)S(1)} %get-tuple-element.531), kind=kOutput, calls=%fused_computation.55.clone.1 | convolution fusion | flops 1762209792 | bytes 3772416 | tf_op jit(solution)/shard_map/while/body/eval_jaxpr/dot_general | solution.py:117
  100.5 2.2 %convolution_add_fusion.5 = f32[224,640]{1,0:T(8,128)S(1)} fusion(f32[224,640]{1,0:T(8,128)S(1)} %get-tuple-element.589, f32[1024,640]{0,1:T(8,128)S(1)} %bitcast.148, s32[1024]{0:T(1024)S(1)} %get-tuple-element.531), kind=kOutput, calls=%fused_computation.55.clone.1 | convolution fusion | flops 1762209792 | bytes 3772416 | tf_op jit(solution)/shard_map/while/body/eval_jaxpr/dot_general | solution.py:117
  104.3 0.8 add.181
  105.2 0.7 add.180
  (139 shorter events, 10.6 us)
Async XLA Ops:
  0.6 4.6 %copy-start = (f32[1,1,3,64,512]{4,3,2,1,0:T(8,128)S(1)}, f32[1,1,3,64,512]{4,3,2,1,0:T(8,128)}, u32[]{:S(2)}) copy-start(f32[1,1,3,64,512]{4,3,2,1,0:T(8,128)} %param.26) | copy-start | bytes 1179652
  0.6 4.8 %copy-start.1 = (f32[1,1,64,512]{3,2,1,0:T(8,128)S(1)}, f32[1,1,64,512]{3,2,1,0:T(8,128)}, u32[]{:S(2)}) copy-start(f32[1,1,64,512]{3,2,1,0:T(8,128)} %param.25) | copy-start | bytes 393220
  2.1 3.4 %copy-start.2 = (f32[512,512,1]{1,0,2:T(8,128)S(1)}, f32[512,512,1]{1,0,2:T(8,128)}, u32[]{:S(2)}) copy-start(f32[512,512,1]{1,0,2:T(8,128)} %constant.365) | copy-start | bytes 3145732
  4.4 2.3 %copy-start.4 = (f32[512,512,1]{1,0,2:T(8,128)S(1)}, f32[512,512,1]{1,0,2:T(8,128)}, u32[]{:S(2)}) copy-start(f32[512,512,1]{1,0,2:T(8,128)} %constant.366) | copy-start | bytes 3145732
  5.4 2.3 %copy-start.3 = (f32[512,512,1]{1,0,2:T(8,128)S(1)}, f32[512,512,1]{1,0,2:T(8,128)}, u32[]{:S(2)}) copy-start(f32[512,512,1]{1,0,2:T(8,128)} %constant.367) | copy-start | bytes 3145732
  7.7 1.3 %copy-start.7 = (f32[8,64]{1,0:T(8,128)S(1)}, f32[8,64]{1,0:T(8,128)}, u32[]{:S(2)}) copy-start(f32[8,64]{1,0:T(8,128)} %constant.364) | copy-start | bytes 6148
  9.8 0.8 copy-start.6
  9.8 0.8 copy-start.8
  29.8 11.4 %copy-start.5 = (s32[1,1,2,1024]{3,2,1,0:T(2,128)S(1)}, s32[1,1,2,1024]{3,2,1,0:T(2,128)}, u32[]{:S(2)}) copy-start(s32[1,1,2,1024]{3,2,1,0:T(2,128)} %param.30) | copy-start | bytes 24580
  29.8 11.4 %copy-start.9 = (s32[1,1,2]{2,1,0:T(1,128)S(1)}, s32[1,1,2]{2,1,0:T(1,128)}, u32[]{:S(2)}) copy-start(s32[1,1,2]{2,1,0:T(1,128)} %param.31) | copy-start | bytes 28
  29.8 52.4 %all-to-all-start = ((f32[32,1,5,5,1024]{4,1,3,2,0:T(1,128)}), f32[32,1,5,5,1024]{4,1,3,2,0:T(1,128)}, u32[]{:S(2)}, u32[]{:S(2)}) async-start(f32[32,1,5,5,1024]{4,1,3,2,0:T(1,128)} %stack.9), calls=%async_computation | async-start | bytes 6553600 | tf_op jit(solution)/shard_map/all_to_all | solution.py:171
  47.7 10.6 %collective-permute-start = (f32[5,1,1024]{2,0,1:T(8,128)S(1)}, f32[5,1,1024]{2,0,1:T(8,128)S(1)}, u32[]{:S(2)}, u32[]{:S(2)}) collective-permute-start(f32[5,1,1024]{2,0,1:T(8,128)S(1)} %get-tuple-element.395), channel_id=1, source_target_pairs={{0,32},{32,64},{64,96},{96,128},{128,160},{160,192},{192,224},{224... | collective-permute-start | bytes 61448 | tf_op jit(solution)/shard_map/ppermute | solution.py:19
  49.7 9.5 %collective-permute-start.1 = (f32[5,1,1024]{2,0,1:T(8,128)S(1)}, f32[5,1,1024]{2,0,1:T(8,128)S(1)}, u32[]{:S(2)}, u32[]{:S(2)}) collective-permute-start(f32[5,1,1024]{2,0,1:T(8,128)S(1)} %get-tuple-element.396), channel_id=1, source_target_pairs={{32,0},{64,32},{96,64},{128,96},{160,128},{192,160},{224,192},{256... | collective-permute-start | bytes 61448 | tf_op jit(solution)/shard_map/ppermute | solution.py:21
